TPU v7x, 32 devices: a whole 2x2x4 slice. The times are simulated.
32 devices in a mesh: row: 4 (over z), col: 8 (over y, x, core).
Axes of the slice: x: 2, y: 2, z: 4, core: 2. Of those that a mesh axis runs over, the one named last changes fastest.
Arguments:
- prior: float32 [4096, 4096], P('row', 'col'), may hold values from -6 to 6, as said below
- observed: int32 [512], replicated, may hold values from 0 to 4095, as said below
- obs_noise: float32 [512], replicated, may hold values from 0.25 to 1
Outputs:
- posterior: float32 [4096, 4096], P('row', 'col')
Inputs may be any that keep to these rules, and one draw needn't show every extreme that they name: prior is symmetric positive semidefinite, and exactly symmetric: prior[i, j] equals prior[j, i] bit for bit. States may repeat; the largest and smallest states of the range are observed in every draw.
All inputs are finite; a program needn't handle non-finite values.
Results may differ from a plain program's by a relative error of at most 0.00012.
Values sent between devices are 32-bit elements; how exact they have to be, the bound alone decides.
A program may use at most 128 MiB of HBM per device.

v0:
```python
import functools

import jax
import jax.numpy as jnp
from jax import lax
from jax.experimental import pallas as pl
from jax.experimental.pallas import tpu as pltpu
from jax.sharding import PartitionSpec as P

F32 = jnp.float32
BF16 = jnp.bfloat16
HI = lax.Precision.HIGHEST
MESH = pl.DeviceIdType.MESH
VMEM = pl.BlockSpec(memory_space=pltpu.VMEM)
LIMIT = 60 * 1024 * 1024


def parts3(x):
    first = x.astype(BF16)
    rest = x - first.astype(F32)
    second = rest.astype(BF16)
    third = (rest - second.astype(F32)).astype(BF16)
    return first, second, third


def dot(a, b):
    return jnp.dot(a, b, preferred_element_type=F32)


def pick_kernel(prior_ref, obs_col_ref, obs_row_ref, s_ref, a_ref, b_ref, one_ref):
    rows, cols = prior_ref.shape
    obs = obs_row_ref.shape[1]
    row_start = lax.axis_index("row") * rows
    col_start = lax.axis_index("col") * cols
    in_cols = lax.broadcasted_iota(jnp.int32, (cols, obs), 0) == obs_row_ref[...] - col_start
    one_ref[...] = jnp.where(in_cols, 1.0, 0.0).astype(BF16)
    tile = 256

    @pl.loop(0, rows // tile)
    def _(t):
        at = pl.ds(pl.multiple_of(t * tile, tile), tile)
        block = prior_ref[at, :]
        p1, p2, p3 = parts3(block)
        pick = one_ref[...]
        a_ref[at, :] = dot(p1, pick) + dot(p2, pick) + dot(p3, pick)
        local = obs_col_ref[...] - (row_start + t * tile)
        left = (lax.broadcasted_iota(jnp.int32, (obs, tile), 1) == local)
        left = jnp.where(left, 1.0, 0.0).astype(BF16)
        got = dot(left, p1) + dot(left, p2) + dot(left, p3)

        @pl.when(t == 0)
        def _():
            b_ref[...] = got

        @pl.when(t > 0)
        def _():
            b_ref[...] += got

    half = obs // 2

    @pl.loop(0, 2)
    def _(t):
        at = pl.ds(pl.multiple_of(t * half, half), half)
        g1, g2, g3 = parts3(b_ref[at, :])
        pick = one_ref[...]
        s_ref[at, :] = dot(g1, pick) + dot(g2, pick) + dot(g3, pick)


def pick_local(prior, observed):
    rows, cols = prior.shape
    obs = observed.shape[0]
    return pl.pallas_call(
        pick_kernel,
        name="pick_local",
        out_shape=(
            jax.ShapeDtypeStruct((obs, obs), F32),
            jax.ShapeDtypeStruct((rows, obs), F32),
            jax.ShapeDtypeStruct((obs, cols), F32),
        ),
        in_specs=[VMEM] * 3,
        out_specs=(VMEM,) * 3,
        scratch_shapes=[pltpu.VMEM((cols, obs), BF16)],
        compiler_params=pltpu.CompilerParams(vmem_limit_bytes=LIMIT),
    )(prior, observed[:, None], observed[None, :])


def bits(size):
    return list(range(size.bit_length() - 1))


def partner(axis, bit):
    me = lax.axis_index(axis)
    one = (me // (1 << bit)) % 2
    return one, {axis: me + (1 - 2 * one) * (1 << bit)}


def greet(axes):
    barrier = pltpu.get_barrier_semaphore()
    for axis, bit in axes:
        _, peer = partner(axis, bit)
        pl.semaphore_signal(barrier, inc=1, device_id=peer, device_id_type=MESH)
    pl.semaphore_wait(barrier, len(axes))


def phases(src, out, acc, recv, send_sem, recv_sem, first_sem, rows, lanes, halving, whole):
    lane = pl.ds(lanes[0], lanes[1])
    state = {"off": 0, "n": rows, "live": src, "path": []}
    result = []
    sem = first_sem

    def at(off, n):
        return pl.ds(pl.multiple_of(off, 8), n)

    for index, (axis, bit) in enumerate(halving):
        def start(axis=axis, bit=bit, index=index, sem=sem):
            one, peer = partner(axis, bit)
            n = state["n"] // 2
            keep = state["off"] + one * n
            give = state["off"] + (1 - one) * n
            copy = pltpu.make_async_remote_copy(
                state["live"].at[at(give, n), lane], recv[index], send_sem.at[sem], recv_sem.at[sem],
                device_id=peer, device_id_type=MESH)
            copy.start()
            state["path"].append((keep, n, peer))
            state["off"], state["n"], state["copy"] = keep, n, copy

        def finish(index=index):
            state["copy"].wait()
            where = at(state["off"], state["n"])
            acc[where, lane] = state["live"][where, lane] + recv[index][...]
            state["live"] = acc

        result.append((start, finish))
        sem += 1
    for index, (axis, bit) in enumerate(whole):
        def start(axis=axis, bit=bit, index=index, sem=sem):
            _, peer = partner(axis, bit)
            where = at(state["off"], state["n"])
            copy = pltpu.make_async_remote_copy(
                acc.at[where, lane], recv[len(halving) + index], send_sem.at[sem], recv_sem.at[sem],
                device_id=peer, device_id_type=MESH)
            copy.start()
            state["copy"] = copy

        def finish(index=index):
            state["copy"].wait()
            where = at(state["off"], state["n"])
            acc[where, lane] = acc[where, lane] + recv[len(halving) + index][...]

        result.append((start, finish))
        sem += 1
    for index in range(len(halving)):
        def start(index=index, sem=sem):
            keep, n, peer = state["path"][len(halving) - 1 - index]
            where = at(keep, n)
            if index == 0:
                out[where, lane] = acc[where, lane]
            copy = pltpu.make_async_remote_copy(
                out.at[where, lane], out.at[where, lane], send_sem.at[sem], recv_sem.at[sem],
                device_id=peer, device_id_type=MESH)
            copy.start()
            state["copy"] = copy

        def finish():
            state["copy"].wait()

        result.append((start, finish))
        sem += 1
    return result


def orders(col_bits):
    return [col_bits, col_bits[:1] + col_bits[1:][::-1]]


def recv_shapes(rows, width, halving, whole):
    shapes = []
    for _ in range(halving):
        rows //= 2
        shapes.append(pltpu.VMEM((rows, width), F32))
    return shapes + [pltpu.VMEM((rows, width), F32)] * whole


def innovation_kernel(col_bits, row_bits, part_ref, out_ref, acc, *rest):
    send_sem, recv_sem = rest[-2:]
    bufs = rest[:-2]
    obs = part_ref.shape[0]
    streams = orders(col_bits)
    width = obs // len(streams)
    each = len(bufs) // len(streams)
    steps = 2 * len(col_bits) + len(row_bits)
    greet([("col", b) for b in col_bits] + [("row", b) for b in row_bits])
    plans = [
        phases(part_ref, out_ref, acc, bufs[i * each:(i + 1) * each], send_sem, recv_sem, i * steps, obs,
               (i * width, width), [("col", b) for b in order], [("row", b) for b in row_bits])
        for i, order in enumerate(streams)
    ]
    for step in range(steps):
        for plan in plans:
            plan[step][0]()
        for plan in plans:
            plan[step][1]()


def reduce_innovation(part, mesh):
    obs = part.shape[0]
    col_bits, row_bits = bits(mesh.shape["col"]), bits(mesh.shape["row"])
    steps = 2 * len(col_bits) + len(row_bits)
    return pl.pallas_call(
        functools.partial(innovation_kernel, col_bits, row_bits),
        name="reduce_innovation",
        out_shape=jax.ShapeDtypeStruct((obs, obs), F32),
        in_specs=[VMEM],
        out_specs=VMEM,
        scratch_shapes=[pltpu.VMEM((obs, obs), F32)]
        + recv_shapes(obs, obs // 2, len(col_bits), len(row_bits)) * 2
        + [pltpu.SemaphoreType.DMA((2 * steps,)), pltpu.SemaphoreType.DMA((2 * steps,))],
        compiler_params=pltpu.CompilerParams(collective_id=0, has_side_effects=True, vmem_limit_bytes=LIMIT),
    )(part)


def row_of(x, k):
    return jnp.broadcast_to(x[k:k + 1, :], x.shape)


def factor_block(d, m):
    size = d.shape[0]
    sub = lax.broadcasted_iota(jnp.int32, (8, size), 0)
    lane = lax.broadcasted_iota(jnp.int32, (8, size), 1)
    done = []
    for mb in range(size // 8):
        panel, right = d[:8], m[:8]
        cols = [jnp.broadcast_to(panel[:, 8 * mb + j:8 * mb + j + 1], (8, size)) for j in range(8)]
        for k in range(8):
            inv = lax.rsqrt(row_of(cols[k], k))
            low = jnp.where(sub > k, cols[k] * inv, 0.0)
            up, um = row_of(panel, k) * inv, row_of(right, k) * inv
            panel = jnp.where(sub == k, up, panel - low * up)
            right = jnp.where(sub == k, um, right - low * um)
            for j in range(k + 1, 8):
                cols[j] = cols[j] - low * row_of(low, j)
        done.append(right)
        if mb + 1 < size // 8:
            both = jnp.concatenate([panel, right], axis=1)
            step = lax.dot_general(panel, both, (((0,), (0,)), ((), ())), precision=HI, preferred_element_type=F32)
            step = step[8 * (mb + 1):]
            d = d[8:] - step[:, :size]
            m = m[8:] - step[:, size:]
    return jnp.concatenate(done, axis=0)


def factor_kernel(s_ref, noise_ref, inv_ref, sm):
    obs = s_ref.shape[0]
    nb = 128
    i = lax.broadcasted_iota(jnp.int32, (obs, obs), 0)
    j = lax.broadcasted_iota(jnp.int32, (obs, obs), 1)
    sm[:, :obs] = s_ref[...] + jnp.where(i == j, noise_ref[...], 0.0)
    sm[:, obs:] = jnp.where(i == j, 1.0, 0.0)
    eye = jnp.where(i[:nb, :nb] == j[:nb, :nb], 1.0, 0.0).astype(F32)
    wide = lax.broadcasted_iota(jnp.int32, (nb, obs), 1)

    @pl.loop(0, obs // nb)
    def _(kb):
        at = pl.ds(pl.multiple_of(kb * nb, nb), nb)
        linv = factor_block(sm[at, at], eye)
        row = jnp.dot(linv, sm[at, :], precision=HI, preferred_element_type=F32)
        inv_ref[at, :] = row[:, obs:]
        below = jnp.where(wide >= (kb + 1) * nb, row[:, :obs], 0.0)
        sm[...] -= lax.dot_general(below, row, (((0,), (0,)), ((), ())), precision=HI, preferred_element_type=F32)


def factor_inverse(s, noise):
    obs = s.shape[0]
    return pl.pallas_call(
        factor_kernel,
        name="factor_inverse",
        out_shape=jax.ShapeDtypeStruct((obs, obs), F32),
        in_specs=[VMEM, VMEM],
        out_specs=VMEM,
        scratch_shapes=[pltpu.VMEM((obs, 2 * obs), F32)],
        compiler_params=pltpu.CompilerParams(vmem_limit_bytes=LIMIT),
        cost_estimate=pl.CostEstimate(flops=4 * obs * obs * obs, bytes_accessed=obs * obs * 8, transcendentals=obs),
    )(s, noise[None, :])


def local(mesh, prior, observed, obs_noise):
    s_part, a_part, b_part = pick_local(prior, observed)
    s = reduce_innovation(s_part, mesh)
    a = lax.psum(a_part, "col")
    b = lax.psum(b_part, "row")
    linv = factor_inverse(s, obs_noise)
    v = jnp.dot(linv, b, precision=HI, preferred_element_type=F32)
    y = jnp.dot(linv.T, v, precision=HI, preferred_element_type=F32)
    return prior - jnp.dot(a, y, precision=HI, preferred_element_type=F32)


def solution(mesh):
    return jax.shard_map(
        functools.partial(local, mesh),
        mesh=mesh,
        in_specs=(P("row", "col"), P(), P()),
        out_specs=P("row", "col"),
        check_vma=False,
    )
```

profile of v0, /device:TPU:0, one launch (start us, length us, event | category | flops | bytes accessed | tf_op | source)
XLA Modules:
  0.0 155.6 jit_solution(2273880079958389046)
XLA Ops:
  6.5 0.0 all-reduce.5.cloned.1.call-start
  6.5 1.5 copy.4.obs_col_ref
  8.1 8.7 %pick_local.1 = (f32[512,512]{1,0:T(8,128)}, f32[1024,512]{1,0:T(8,128)}, f32[512,512]{1,0:T(8,128)}) custom-call(f32[1024,512]{1,0:T(8,128)} %prior_ref.1, s32[512,1]{1,0:T(8,128)} %copy.4.obs_col_ref, s32[1,512]{1,0:T(1,128)} %bitcast.10), custom_call_target="tpu_custom_call" | custom-call | tf_op jit(solution)/shard_map/pick_local/pallas_call | solution.py:72
  16.8 0.0 all-reduce.5.cloned.1.call-update
  16.8 0.0 all-reduce.3.cloned.1.call-start
  16.9 0.7 all-reduce.3.cloned.1.call-update
  17.6 46.3 %reduce_innovation.1.s_ref = f32[512,512]{1,0:T(8,128)} custom-call(f32[512,512]{1,0:T(8,128)} %get-tuple-element.9.part_ref), custom_call_target="tpu_custom_call" | custom-call | tf_op jit(solution)/shard_map/reduce_innovation/pallas_call | solution.py:209
  63.8 45.4 %factor_inverse.1 = f32[512,512]{1,0:T(8,128)} custom-call(f32[512,512]{1,0:T(8,128)} %reduce_innovation.1.s_ref, f32[1,512]{1,0:T(1,128)} %bitcast.11), custom_call_target="tpu_custom_call" | custom-call | flops 536870912 | bytes 2097152 | tf_op jit(solution)/shard_map/factor_inverse/pallas_call | solution.py:274
  109.2 0.0 copy-start
  109.2 0.0 all-reduce.5.cloned.1.call-done
  109.3 3.5 %fusion = f32[512,512]{1,0:T(8,128)S(1)} fusion(f32[512,512]{1,0:T(8,128)} %factor_inverse.1, f32[512,512]{1,0:T(8,128)} %all-reduce.5.cloned.1.call-done), kind=kOutput, calls=%fused_computation.1 | convolution fusion | flops 1610612736 | bytes 3145728 | tf_op jit(solution)/shard_map/dot_general | solution.py:292
  112.8 0.0 copy-done
  112.8 0.0 copy-start.1
  112.8 2.9 %fusion.1 = f32[512,512]{1,0:T(8,128)} fusion(f32[512,512]{1,0:T(8,128)S(1)} %copy-done, f32[512,512]{1,0:T(8,128)S(1)} %fusion), kind=kOutput, calls=%fused_computation.2 | convolution fusion | flops 1610612736 | bytes 3145728 | tf_op jit(solution)/shard_map/dot_general | solution.py:293
  115.7 26.4 %all-reduce.3.cloned.1.call-done = f32[1024,512]{1,0:T(8,128)} async-done(((f32[1024,512]{1,0:T(8,128)}), f32[1024,512]{1,0:T(8,128)}) %all-reduce.3.cloned.1.call-update) | async-done | bytes 2097168 | tf_op jit(solution)/shard_map/psum | solution.py:289
  142.1 0.0 copy-done.1
  142.1 6.6 %convolution_subtract_fusion = f32[1024,512]{1,0:T(8,128)} fusion(f32[1024,512]{1,0:T(8,128)S(1)} %copy-done.1, f32[1024,512]{1,0:T(8,128)} %all-reduce.3.cloned.1.call-done, f32[512,512]{1,0:T(8,128)} %fusion.1), kind=kOutput, calls=%fused_computation | convolution fusion | flops 3221749760 | bytes 7340032 | tf_op jit(solution)/shard_map/dot_general | solution.py:294
Async XLA Ops:
  6.5 102.7 %all-reduce.5.cloned.1.call-start = ((), (), s32[]{:S(2)}) async-start(), calls=%async_computation.1 | async-start | bytes 2097152 | tf_op jit(solution)/shard_map/psum | solution.py:290
  16.8 125.3 %all-reduce.3.cloned.1.call-start = ((), (), s32[]{:S(2)}) async-start(), calls=%async_computation | async-start | bytes 4194304 | tf_op jit(solution)/shard_map/psum | solution.py:289
  109.2 3.5 %copy-start = (f32[512,512]{1,0:T(8,128)S(1)}, f32[512,512]{1,0:T(8,128)}, u32[]{:S(2)}) copy-start(f32[512,512]{1,0:T(8,128)} %factor_inverse.1) | copy-start | bytes 3145732
  112.8 29.3 %copy-start.1 = (f32[1024,512]{1,0:T(8,128)S(1)}, f32[1024,512]{1,0:T(8,128)}, u32[]{:S(2)}) copy-start(f32[1024,512]{1,0:T(8,128)} %prior_ref.1) | copy-start | bytes 6291460
Sparse Core Ops, SparseCore 0:
  16.9 60.5 all-reduce.4
  80.7 61.3 all-reduce.2
where the time goes:
time: 156 us
  Pallas kernels  100 us (64%)
  waiting for transfers between devices  27.2 us (17%)
  between operations  13.5 us (9%)
  matrix products  13 us (8%)
    pallas_call x1, Pallas kernels, reduce_innovation(): pl.pallas_call(functools.partial(innovation_kernel, col_bits, row_bits),...  46.3 us
    pallas_call x1, Pallas kernels, factor_inverse(): pl.pallas_call(factor_kernel, name='factor_inverse', out_shape=jax.ShapeD...  45.4 us
    psum x1, waiting for transfers between devices, local(): a = lax.psum(a_part, 'col')  26.4 us
    pallas_call x1, Pallas kernels, pick_local(): pl.pallas_call(pick_kernel, name='pick_local', out_shape=(jax.ShapeDtypeS...  8.72 us
    dot_general x1, matrix products, local(): return prior - jnp.dot(a, y, precision=HI, preferred_element_type=F32)  6.61 us
    dot_general x1, matrix products, local(): v = jnp.dot(linv, b, precision=HI, preferred_element_type=F32)  3.5 us
  transfers between devices with their start and end apart: 2, of which 1 were waited for; matrix products, arithmetic and copies ran while one was open for 4% of the time, Pallas kernels for 59%

commit v1 on v0

v1 whole, which is shorter than its diff:
```python
import functools

import jax
import jax.numpy as jnp
from jax import lax
from jax.experimental import pallas as pl
from jax.experimental.pallas import tpu as pltpu
from jax.sharding import PartitionSpec as P

F32 = jnp.float32
BF16 = jnp.bfloat16
HI = lax.Precision.HIGHEST
MID = lax.Precision.HIGH
MESH = pl.DeviceIdType.MESH
VMEM = pl.BlockSpec(memory_space=pltpu.VMEM)
LIMIT = 60 * 1024 * 1024


def parts3(x):
    first = x.astype(BF16)
    rest = x - first.astype(F32)
    second = rest.astype(BF16)
    third = (rest - second.astype(F32)).astype(BF16)
    return first, second, third


def dot(a, b):
    return jnp.dot(a, b, preferred_element_type=F32)


def pick_kernel(prior_ref, obs_col_ref, obs_row_ref, s_ref, a_ref, b_ref, one_ref):
    rows, cols = prior_ref.shape
    obs = obs_row_ref.shape[1]
    row_start = lax.axis_index("row") * rows
    col_start = lax.axis_index("col") * cols
    in_cols = lax.broadcasted_iota(jnp.int32, (cols, obs), 0) == obs_row_ref[...] - col_start
    one_ref[...] = jnp.where(in_cols, 1.0, 0.0).astype(BF16)
    tile = 256

    @pl.loop(0, rows // tile)
    def _(t):
        at = pl.ds(pl.multiple_of(t * tile, tile), tile)
        block = prior_ref[at, :]
        p1, p2, p3 = parts3(block)
        pick = one_ref[...]
        a_ref[at, :] = dot(p1, pick) + dot(p2, pick) + dot(p3, pick)
        local = obs_col_ref[...] - (row_start + t * tile)
        left = (lax.broadcasted_iota(jnp.int32, (obs, tile), 1) == local)
        left = jnp.where(left, 1.0, 0.0).astype(BF16)
        got = dot(left, p1) + dot(left, p2) + dot(left, p3)

        @pl.when(t == 0)
        def _():
            b_ref[...] = got

        @pl.when(t > 0)
        def _():
            b_ref[...] += got

    half = obs // 2

    @pl.loop(0, 2)
    def _(t):
        at = pl.ds(pl.multiple_of(t * half, half), half)
        g1, g2, g3 = parts3(b_ref[at, :])
        pick = one_ref[...]
        s_ref[at, :] = dot(g1, pick) + dot(g2, pick) + dot(g3, pick)


def pick_local(prior, observed):
    rows, cols = prior.shape
    obs = observed.shape[0]
    return pl.pallas_call(
        pick_kernel,
        name="pick_local",
        out_shape=(
            jax.ShapeDtypeStruct((obs, obs), F32),
            jax.ShapeDtypeStruct((rows, obs), F32),
            jax.ShapeDtypeStruct((obs, cols), F32),
        ),
        in_specs=[VMEM] * 3,
        out_specs=(VMEM,) * 3,
        scratch_shapes=[pltpu.VMEM((cols, obs), BF16)],
        compiler_params=pltpu.CompilerParams(vmem_limit_bytes=LIMIT),
    )(prior, observed[:, None], observed[None, :])


def bits(size):
    return list(range(size.bit_length() - 1))


def partner(axis, bit):
    me = lax.axis_index(axis)
    one = (me // (1 << bit)) % 2
    return one, {axis: me + (1 - 2 * one) * (1 << bit)}


def greet(axes):
    barrier = pltpu.get_barrier_semaphore()
    for axis, bit in axes:
        _, peer = partner(axis, bit)
        pl.semaphore_signal(barrier, inc=1, device_id=peer, device_id_type=MESH)
    pl.semaphore_wait(barrier, len(axes))


def phases(src, out, acc, recv, send_sem, recv_sem, first_sem, lanes, halving, whole):
    lane = pl.ds(lanes[0], lanes[1])
    off, n, live = 0, src.shape[0], src
    result, path = [], []

    def at(off, n):
        return pl.ds(pl.multiple_of(off, 8), n)

    def send(source, target, peer):
        sem = first_sem + len(result)
        return pltpu.make_async_remote_copy(
            source, target, send_sem.at[sem], recv_sem.at[sem], device_id=peer, device_id_type=MESH)

    def reducing(copy, where, live, buf):
        def finish():
            copy.wait()
            acc[where, lane] = live[where, lane] + buf[...]

        result.append((copy.start, finish))

    for axis, bit in halving:
        one, peer = partner(axis, bit)
        n //= 2
        give = at(off + (1 - one) * n, n)
        off = off + one * n
        buf = recv[len(result)]
        reducing(send(live.at[give, lane], buf, peer), at(off, n), live, buf)
        live = acc
        path.append((off, n, peer))
    for axis, bit in whole:
        _, peer = partner(axis, bit)
        buf = recv[len(result)]
        where = at(off, n)
        reducing(send(acc.at[where, lane], buf, peer), where, acc, buf)
    for index, (off, n, peer) in enumerate(path[::-1]):
        where = at(off, n)
        copy = send(out.at[where, lane], out.at[where, lane], peer)

        def start(copy=copy, where=where, first=index == 0):
            if first:
                out[where, lane] = acc[where, lane]
            copy.start()

        result.append((start, copy.wait))
    return result


def orders(col_bits):
    return [col_bits, col_bits[:1] + col_bits[1:][::-1]]


def recv_shapes(rows, width, halving, whole):
    shapes = []
    for _ in range(halving):
        rows //= 2
        shapes.append(pltpu.VMEM((rows, width), F32))
    return shapes + [pltpu.VMEM((rows, width), F32)] * whole


def row_of(x, k):
    return jnp.broadcast_to(x[k:k + 1, :], x.shape)


def factor_block(d, m, tick):
    size = d.shape[0]
    sub = lax.broadcasted_iota(jnp.int32, (8, size), 0)
    lane = lax.broadcasted_iota(jnp.int32, (8, size), 1)
    done = []
    for mb in range(size // 8):
        tick(mb)
        panel, right = d[:8], m[:8]
        cols = [jnp.broadcast_to(panel[:, 8 * mb + j:8 * mb + j + 1], (8, size)) for j in range(8)]
        for k in range(8):
            inv = lax.rsqrt(row_of(cols[k], k))
            low = jnp.where(sub > k, cols[k] * inv, 0.0)
            up, um = row_of(panel, k) * inv, row_of(right, k) * inv
            panel = jnp.where(sub == k, up, panel - low * up)
            right = jnp.where(sub == k, um, right - low * um)
            for j in range(k + 1, 8):
                cols[j] = cols[j] - low * row_of(low, j)
        done.append(right)
        if mb + 1 < size // 8:
            both = jnp.concatenate([panel, right], axis=1)
            step = lax.dot_general(panel, both, (((0,), (0,)), ((), ())), precision=HI, preferred_element_type=F32)
            step = step[8 * (mb + 1):]
            d = d[8:] - step[:, :size]
            m = m[8:] - step[:, size:]
    return jnp.concatenate(done, axis=0)


NB = 128
TICKS = 4


def update_kernel(col_bits, row_bits, s_part, a_part, b_part, noise_ref, inv_ref, a_ref, b_ref, s_ref, sm, *rest):
    send_sem, recv_sem = rest[-2:]
    (s_acc, a_acc, b_acc), bufs = rest[:3], list(rest[3:-2])
    obs = s_part.shape[0]
    col_axes = [[("col", b) for b in order] for order in orders(col_bits)]
    row_axes = [("row", b) for b in row_bits]
    greet(col_axes[0] + row_axes)
    sems = [0]

    def plan(src, out, acc, lanes, halving, whole):
        count = len(halving) + len(whole)
        mine = [bufs.pop(0) for _ in range(count)]
        steps = phases(src, out, acc, mine, send_sem, recv_sem, sems[0], lanes, halving, whole)
        sems[0] += len(steps)
        return steps

    width = obs // 2
    s_plans = [plan(s_part, s_ref, s_acc, (i * width, width), col_axes[i], row_axes) for i in range(2)]
    a_plans = [plan(a_part, a_ref, a_acc, (i * width, width), col_axes[i], []) for i in range(2)]
    b_plan = plan(b_part, b_ref, b_acc, (0, b_part.shape[1]), row_axes, [])

    for step in range(len(s_plans[0])):
        for steps in s_plans:
            steps[step][0]()
        if step == len(col_bits) + len(row_bits):
            b_plan[0][0]()
        for steps in s_plans:
            steps[step][1]()

    total = TICKS * (obs // NB)
    actions = [[] for _ in range(total + 1)]
    for steps, span, begun in [(a_plans[0], total, False), (a_plans[1], total, False), (b_plan, total - 1, True)]:
        if not begun:
            actions[0].append(steps[0][0])
        for index in range(len(steps)):
            slot = actions[round(span * (index + 1) / len(steps))]
            slot.append(steps[index][1])
            if index + 1 < len(steps):
                slot.append(steps[index + 1][0])

    i = lax.broadcasted_iota(jnp.int32, (obs, obs), 0)
    j = lax.broadcasted_iota(jnp.int32, (obs, obs), 1)
    sm[:, :obs] = s_ref[...] + jnp.where(i == j, noise_ref[...], 0.0)
    sm[:, obs:] = jnp.where(i == j, 1.0, 0.0)
    eye = jnp.where(i[:NB, :NB] == j[:NB, :NB], 1.0, 0.0).astype(F32)
    wide = lax.broadcasted_iota(jnp.int32, (NB, obs), 1)

    @pl.loop(0, obs // NB)
    def _(kb):
        def tick(mb):
            if mb % (NB // 8 // TICKS):
                return
            for block in range(obs // NB):
                todo = actions[block * TICKS + mb // (NB // 8 // TICKS)]
                if todo:
                    @pl.when(kb == block)
                    def _():
                        for act in todo:
                            act()

        at = pl.ds(pl.multiple_of(kb * NB, NB), NB)
        linv = factor_block(sm[at, at], eye, tick)
        row = jnp.dot(linv, sm[at, :], precision=HI, preferred_element_type=F32)
        inv_ref[at, :] = row[:, obs:]
        below = jnp.where(wide >= (kb + 1) * NB, row[:, :obs], 0.0)
        sm[...] -= lax.dot_general(below, row, (((0,), (0,)), ((), ())), precision=HI, preferred_element_type=F32)

    for act in actions[total]:
        act()


def update_parts(s_part, a_part, b_part, noise, mesh):
    obs = s_part.shape[0]
    col_bits, row_bits = bits(mesh.shape["col"]), bits(mesh.shape["row"])
    nc, nr = len(col_bits), len(row_bits)
    copies = 2 * (2 * nc + nr) + 2 * 2 * nc + 2 * nr
    like = jax.ShapeDtypeStruct
    return pl.pallas_call(
        functools.partial(update_kernel, col_bits, row_bits),
        name="update_parts",
        out_shape=(like((obs, obs), F32), like(a_part.shape, F32), like(b_part.shape, F32)),
        in_specs=[VMEM] * 4,
        out_specs=(VMEM,) * 3,
        scratch_shapes=[
            pltpu.VMEM((obs, obs), F32),
            pltpu.VMEM((obs, 2 * obs), F32),
            pltpu.VMEM(s_part.shape, F32),
            pltpu.VMEM(a_part.shape, F32),
            pltpu.VMEM(b_part.shape, F32),
        ]
        + recv_shapes(obs, obs // 2, nc, nr) * 2
        + recv_shapes(a_part.shape[0], obs // 2, nc, 0) * 2
        + recv_shapes(obs, b_part.shape[1], nr, 0)
        + [pltpu.SemaphoreType.DMA((copies,)), pltpu.SemaphoreType.DMA((copies,))],
        compiler_params=pltpu.CompilerParams(collective_id=0, has_side_effects=True, vmem_limit_bytes=LIMIT),
    )(s_part, a_part, b_part, noise[None, :])


def local(mesh, prior, observed, obs_noise):
    s_part, a_part, b_part = pick_local(prior, observed)
    linv, a, b = update_parts(s_part, a_part, b_part, obs_noise, mesh)
    v = jnp.dot(linv, b, precision=MID, preferred_element_type=F32)
    y = jnp.dot(linv.T, v, precision=MID, preferred_element_type=F32)
    return prior - jnp.dot(a, y, precision=MID, preferred_element_type=F32)


def solution(mesh):
    return jax.shard_map(
        functools.partial(local, mesh),
        mesh=mesh,
        in_specs=(P("row", "col"), P(), P()),
        out_specs=P("row", "col"),
        check_vma=False,
    )
```

time: 156 us -> 109 us (0.70)
  waiting for transfers between devices: 27.2 us -> 0 us
  between operations: 13.5 us -> 0.07 us
  matrix products: 13 us -> 6.97 us
    psum x2 -> x0, waiting for transfers between devices: 26.5 us -> none  [the longest x1 26.4 us: local(): a = lax.psum(a_part, 'col')]
    dot_general x3, matrix products: 13 us -> 6.97 us  [the longest x1 3.26 us: local(): return prior - jnp.dot(a, y, precision=MID, preferred_element_type=F32)]
    pallas_call x2 -> x1, Pallas kernels: 91.7 us -> 91.2 us  [update_parts(): pl.pallas_call(functools.partial(update_kernel, col_bits, row_bits), name...]
  transfers between devices with their start and end apart: 2 -> 0, of which waited for: 1 -> 0; matrix products, arithmetic and copies ran while one was open for 4% -> 0% of each run, Pallas kernels for 59% -> 0%
where the time goes in v1:
time: 109 us
  Pallas kernels  99.9 us (92%)
  matrix products  6.97 us (6%)
  local copies, waits for them, and re-layouts  2.08 us (2%)
    pallas_call x1, Pallas kernels, update_parts(): pl.pallas_call(functools.partial(update_kernel, col_bits, row_bits), name...  91.2 us
    pallas_call x1, Pallas kernels, pick_local(): pl.pallas_call(pick_kernel, name='pick_local', out_shape=(jax.ShapeDtypeS...  8.73 us
    dot_general x1, matrix products, local(): return prior - jnp.dot(a, y, precision=MID, preferred_element_type=F32)  3.26 us
    dot_general x1, matrix products, local(): v = jnp.dot(linv, b, precision=MID, preferred_element_type=F32)  2.69 us

profile of v1, /device:TPU:0, one launch (start us, length us, event | category | flops | bytes accessed | tf_op | source)
XLA Modules:
  0.0 109.0 jit_solution(16977207870168601901)
XLA Ops:
  0.0 1.5 %copy.4.obs_col_ref = s32[512,1]{1,0:T(8,128)} copy(s32[512,1]{0,1:T(1,128)} %bitcast.9) | data formatting | bytes 4096 | tf_op jit(solution)/shard_map/broadcast_in_dim | solution.py:85
  1.5 8.7 %pick_local.1 = (f32[512,512]{1,0:T(8,128)}, f32[1024,512]{1,0:T(8,128)}, f32[512,512]{1,0:T(8,128)}) custom-call(f32[1024,512]{1,0:T(8,128)} %prior_ref.1, s32[512,1]{1,0:T(8,128)} %copy.4.obs_col_ref, s32[1,512]{1,0:T(1,128)} %bitcast.10), custom_call_target="tpu_custom_call" | custom-call | tf_op jit(solution)/shard_map/pick_local/pallas_call | solution.py:73
  10.3 91.2 %update_parts.1 = (f32[512,512]{1,0:T(8,128)}, f32[1024,512]{1,0:T(8,128)}, f32[512,512]{1,0:T(8,128)}) custom-call(f32[512,512]{1,0:T(8,128)} %get-tuple-element.11.s_part, f32[1024,512]{1,0:T(8,128)} %get-tuple-element.12.a_part, f32[512,512]{1,0:T(8,128)} %get-tuple-element.13.b_part, f32[1,512]{1,0:T(1,128)} %bitcast.11), custom_call_target="tpu_custom_call" | custom-call | tf_op jit(solution)/shard_map/update_parts/pallas_call | solution.py:277
  101.5 0.0 copy-start.1
  101.5 0.0 copy-start.2
  101.5 2.7 %fusion = f32[512,512]{1,0:T(8,128)S(1)} fusion(f32[512,512]{1,0:T(8,128)} %get-tuple-element.15, f32[512,512]{1,0:T(8,128)} %get-tuple-element.16), kind=kOutput, calls=%fused_computation.1 | convolution fusion | flops 805306368 | bytes 3145728 | tf_op jit(solution)/shard_map/dot_general | solution.py:301
  104.2 0.0 copy-done.1
  104.2 0.0 copy-start
  104.2 1.0 fusion.1
  105.2 0.0 copy-done.2
  105.2 0.5 copy-done
  105.8 3.3 %convolution_subtract_fusion = f32[1024,512]{1,0:T(8,128)} fusion(f32[1024,512]{1,0:T(8,128)S(1)} %copy-done, f32[1024,512]{1,0:T(8,128)S(1)} %copy-done.2, f32[512,512]{1,0:T(8,128)S(1)} %fusion.1), kind=kOutput, calls=%fused_computation | convolution fusion | flops 1611137024 | bytes 7340032 | tf_op jit(solution)/shard_map/dot_general | solution.py:303
Async XLA Ops:
  101.5 2.7 %copy-start.1 = (f32[512,512]{1,0:T(8,128)S(1)}, f32[512,512]{1,0:T(8,128)}, u32[]{:S(2)}) copy-start(f32[512,512]{1,0:T(8,128)} %get-tuple-element.15) | copy-start | bytes 3145732
  101.5 3.8 %copy-start.2 = (f32[1024,512]{1,0:T(8,128)S(1)}, f32[1024,512]{1,0:T(8,128)}, u32[]{:S(2)}) copy-start(f32[1024,512]{1,0:T(8,128)} %get-tuple-element.14) | copy-start | bytes 6291460
  104.2 1.6 %copy-start = (f32[1024,512]{1,0:T(8,128)S(1)}, f32[1024,512]{1,0:T(8,128)}, u32[]{:S(2)}) copy-start(f32[1024,512]{1,0:T(8,128)} %prior_ref.1) | copy-start | bytes 6291460

commit v2 on v1

--- a/solution.py
+++ b/solution.py
@@ -28,24 +28,23 @@
     return jnp.dot(a, b, preferred_element_type=F32)
 
 
-def pick_kernel(prior_ref, obs_col_ref, obs_row_ref, s_ref, a_ref, b_ref, one_ref):
+TILE = 256
+
+
+def pick_rows(prior_ref, obs_ref, one_ref, s_ref, b_ref):
     rows, cols = prior_ref.shape
-    obs = obs_row_ref.shape[1]
+    obs = obs_ref.shape[1]
     row_start = lax.axis_index("row") * rows
     col_start = lax.axis_index("col") * cols
-    in_cols = lax.broadcasted_iota(jnp.int32, (cols, obs), 0) == obs_row_ref[...] - col_start
+    in_cols = lax.broadcasted_iota(jnp.int32, (cols, obs), 0) == obs_ref[...] - col_start
     one_ref[...] = jnp.where(in_cols, 1.0, 0.0).astype(BF16)
-    tile = 256
-
-    @pl.loop(0, rows // tile)
+    tall = jnp.broadcast_to(obs_ref[...].astype(F32), (8, obs)).T[:, :1].astype(jnp.int32)
+
+    @pl.loop(0, rows // TILE)
     def _(t):
-        at = pl.ds(pl.multiple_of(t * tile, tile), tile)
-        block = prior_ref[at, :]
-        p1, p2, p3 = parts3(block)
-        pick = one_ref[...]
-        a_ref[at, :] = dot(p1, pick) + dot(p2, pick) + dot(p3, pick)
-        local = obs_col_ref[...] - (row_start + t * tile)
-        left = (lax.broadcasted_iota(jnp.int32, (obs, tile), 1) == local)
+        at = pl.ds(pl.multiple_of(t * TILE, TILE), TILE)
+        p1, p2, p3 = parts3(prior_ref[at, :])
+        left = lax.broadcasted_iota(jnp.int32, (obs, TILE), 1) == tall - (row_start + t * TILE)
         left = jnp.where(left, 1.0, 0.0).astype(BF16)
         got = dot(left, p1) + dot(left, p2) + dot(left, p3)
 
@@ -57,32 +56,21 @@
         def _():
             b_ref[...] += got
 
-    half = obs // 2
-
-    @pl.loop(0, 2)
+    @pl.loop(0, obs // TILE)
     def _(t):
-        at = pl.ds(pl.multiple_of(t * half, half), half)
+        at = pl.ds(pl.multiple_of(t * TILE, TILE), TILE)
         g1, g2, g3 = parts3(b_ref[at, :])
         pick = one_ref[...]
         s_ref[at, :] = dot(g1, pick) + dot(g2, pick) + dot(g3, pick)
 
 
-def pick_local(prior, observed):
-    rows, cols = prior.shape
-    obs = observed.shape[0]
-    return pl.pallas_call(
-        pick_kernel,
-        name="pick_local",
-        out_shape=(
-            jax.ShapeDtypeStruct((obs, obs), F32),
-            jax.ShapeDtypeStruct((rows, obs), F32),
-            jax.ShapeDtypeStruct((obs, cols), F32),
-        ),
-        in_specs=[VMEM] * 3,
-        out_specs=(VMEM,) * 3,
-        scratch_shapes=[pltpu.VMEM((cols, obs), BF16)],
-        compiler_params=pltpu.CompilerParams(vmem_limit_bytes=LIMIT),
-    )(prior, observed[:, None], observed[None, :])
+def pick_columns(prior_ref, one_ref, a_ref, first, last):
+    @pl.loop(first, last)
+    def _(t):
+        at = pl.ds(pl.multiple_of(t * TILE, TILE), TILE)
+        p1, p2, p3 = parts3(prior_ref[at, :])
+        pick = one_ref[...]
+        a_ref[at, :] = dot(p1, pick) + dot(p2, pick) + dot(p3, pick)
 
 
 def bits(size):
@@ -168,28 +156,45 @@
 
 def factor_block(d, m, tick):
     size = d.shape[0]
+    tall = size // TICKS
+    tiles = tall // 8
     sub = lax.broadcasted_iota(jnp.int32, (8, size), 0)
-    lane = lax.broadcasted_iota(jnp.int32, (8, size), 1)
     done = []
-    for mb in range(size // 8):
-        tick(mb)
-        panel, right = d[:8], m[:8]
-        cols = [jnp.broadcast_to(panel[:, 8 * mb + j:8 * mb + j + 1], (8, size)) for j in range(8)]
-        for k in range(8):
-            inv = lax.rsqrt(row_of(cols[k], k))
-            low = jnp.where(sub > k, cols[k] * inv, 0.0)
-            up, um = row_of(panel, k) * inv, row_of(right, k) * inv
-            panel = jnp.where(sub == k, up, panel - low * up)
-            right = jnp.where(sub == k, um, right - low * um)
-            for j in range(k + 1, 8):
-                cols[j] = cols[j] - low * row_of(low, j)
+    for hb in range(TICKS):
+        tick(hb)
+        panel = [d[8 * t:8 * t + 8] for t in range(tiles)]
+        right = [m[8 * t:8 * t + 8] for t in range(tiles)]
+        for g in range(tiles):
+            base = hb * tall + 8 * g
+            cols = {
+                (t, j): jnp.broadcast_to(panel[t][:, base + j:base + j + 1], (8, size))
+                for t in range(g, tiles) for j in range(8)
+            }
+            for k in range(8):
+                lead = cols[g, k]
+                inv = lax.rsqrt(row_of(lead, k))
+                inv2 = inv * inv
+                up, um = row_of(panel[g], k) * inv, row_of(right[g], k) * inv
+                ahead = {j: row_of(lead, j) for j in range(k + 1, 8)}
+                for t in range(g, tiles):
+                    scaled = cols[t, k] * inv2
+                    for j in range(k + 1, 8):
+                        cols[t, j] = cols[t, j] - scaled * ahead[j]
+                    low = cols[t, k] * inv
+                    if t == g:
+                        low = jnp.where(sub > k, low, 0.0)
+                    panel[t] = panel[t] - low * up
+                    right[t] = right[t] - low * um
+                panel[g] = jnp.where(sub == k, up, panel[g])
+                right[g] = jnp.where(sub == k, um, right[g])
+        panel, right = jnp.concatenate(panel, axis=0), jnp.concatenate(right, axis=0)
         done.append(right)
-        if mb + 1 < size // 8:
+        if hb + 1 < TICKS:
             both = jnp.concatenate([panel, right], axis=1)
             step = lax.dot_general(panel, both, (((0,), (0,)), ((), ())), precision=HI, preferred_element_type=F32)
-            step = step[8 * (mb + 1):]
-            d = d[8:] - step[:, :size]
-            m = m[8:] - step[:, size:]
+            step = step[tall * (hb + 1):]
+            d = d[tall:] - step[:, :size]
+            m = m[tall:] - step[:, size:]
     return jnp.concatenate(done, axis=0)
 
 
@@ -197,8 +202,10 @@
 TICKS = 4
 
 
-def update_kernel(col_bits, row_bits, s_part, a_part, b_part, noise_ref, inv_ref, a_ref, b_ref, s_ref, sm, *rest):
+def update_kernel(col_bits, row_bits, prior_ref, obs_ref, noise_ref, inv_ref, a_ref, b_ref, s_part, a_part, b_part, one_ref,
+                  s_ref, sm, *rest):
     send_sem, recv_sem = rest[-2:]
+    pick_rows(prior_ref, obs_ref, one_ref, s_part, b_part)
     (s_acc, a_acc, b_acc), bufs = rest[:3], list(rest[3:-2])
     obs = s_part.shape[0]
     col_axes = [[("col", b) for b in order] for order in orders(col_bits)]
@@ -223,6 +230,9 @@
             steps[step][0]()
         if step == len(col_bits) + len(row_bits):
             b_plan[0][0]()
+        if step < 2:
+            half = prior_ref.shape[0] // TILE // 2
+            pick_columns(prior_ref, one_ref, a_part, step * half, (step + 1) * half)
         for steps in s_plans:
             steps[step][1]()
 
@@ -247,10 +257,8 @@
     @pl.loop(0, obs // NB)
     def _(kb):
         def tick(mb):
-            if mb % (NB // 8 // TICKS):
-                return
             for block in range(obs // NB):
-                todo = actions[block * TICKS + mb // (NB // 8 // TICKS)]
+                todo = actions[block * TICKS + mb]
                 if todo:
                     @pl.when(kb == block)
                     def _():
@@ -268,8 +276,8 @@
         act()
 
 
-def update_parts(s_part, a_part, b_part, noise, mesh):
-    obs = s_part.shape[0]
+def update_parts(prior, observed, noise, mesh):
+    (rows, cols), obs = prior.shape, observed.shape[0]
     col_bits, row_bits = bits(mesh.shape["col"]), bits(mesh.shape["row"])
     nc, nr = len(col_bits), len(row_bits)
     copies = 2 * (2 * nc + nr) + 2 * 2 * nc + 2 * nr
@@ -277,27 +285,30 @@
     return pl.pallas_call(
         functools.partial(update_kernel, col_bits, row_bits),
         name="update_parts",
-        out_shape=(like((obs, obs), F32), like(a_part.shape, F32), like(b_part.shape, F32)),
-        in_specs=[VMEM] * 4,
+        out_shape=(like((obs, obs), F32), like((rows, obs), F32), like((obs, cols), F32)),
+        in_specs=[VMEM] * 3,
         out_specs=(VMEM,) * 3,
         scratch_shapes=[
             pltpu.VMEM((obs, obs), F32),
+            pltpu.VMEM((rows, obs), F32),
+            pltpu.VMEM((obs, cols), F32),
+            pltpu.VMEM((cols, obs), BF16),
+            pltpu.VMEM((obs, obs), F32),
             pltpu.VMEM((obs, 2 * obs), F32),
-            pltpu.VMEM(s_part.shape, F32),
-            pltpu.VMEM(a_part.shape, F32),
-            pltpu.VMEM(b_part.shape, F32),
+            pltpu.VMEM((obs, obs), F32),
+            pltpu.VMEM((rows, obs), F32),
+            pltpu.VMEM((obs, cols), F32),
         ]
         + recv_shapes(obs, obs // 2, nc, nr) * 2
-        + recv_shapes(a_part.shape[0], obs // 2, nc, 0) * 2
-        + recv_shapes(obs, b_part.shape[1], nr, 0)
+        + recv_shapes(rows, obs // 2, nc, 0) * 2
+        + recv_shapes(obs, cols, nr, 0)
         + [pltpu.SemaphoreType.DMA((copies,)), pltpu.SemaphoreType.DMA((copies,))],
         compiler_params=pltpu.CompilerParams(collective_id=0, has_side_effects=True, vmem_limit_bytes=LIMIT),
-    )(s_part, a_part, b_part, noise[None, :])
+    )(prior, observed[None, :], noise[None, :])
 
 
 def local(mesh, prior, observed, obs_noise):
-    s_part, a_part, b_part = pick_local(prior, observed)
-    linv, a, b = update_parts(s_part, a_part, b_part, obs_noise, mesh)
+    linv, a, b = update_parts(prior, observed, obs_noise, mesh)
     v = jnp.dot(linv, b, precision=MID, preferred_element_type=F32)
     y = jnp.dot(linv.T, v, precision=MID, preferred_element_type=F32)
     return prior - jnp.dot(a, y, precision=MID, preferred_element_type=F32)

time: 109 us -> 96.8 us (0.89)
  Pallas kernels: 99.9 us -> 89 us
  local copies, waits for them, and re-layouts: 2.08 us -> 0.55 us
    pallas_call x1 -> x0, Pallas kernels: 8.73 us -> none  [pick_local(): pl.pallas_call(pick_kernel, name='pick_local', out_shape=(jax.ShapeDtypeS...]
    pallas_call x1, Pallas kernels: 91.2 us -> 89 us  [update_parts(): pl.pallas_call(functools.partial(update_kernel, col_bits, row_bits), name...]
    broadcast_in_dim x1 -> x0, local copies, waits for them, and re-layouts: 1.52 us -> none  [pick_local(): observed[:, None]]
where the time goes in v2:
time: 96.8 us; the launch traced here: 96.6 us
  Pallas kernels  89 us (92%)
  matrix products  6.98 us (7%)
    pallas_call x1, Pallas kernels, update_parts(): pl.pallas_call(functools.partial(update_kernel, col_bits, row_bits), name...  89 us
    dot_general x1, matrix products, local(): return prior - jnp.dot(a, y, precision=MID, preferred_element_type=F32)  3.26 us
    dot_general x1, matrix products, local(): v = jnp.dot(linv, b, precision=MID, preferred_element_type=F32)  2.69 us

profile of v2, /device:TPU:0, one launch (start us, length us, event | category | flops | bytes accessed | tf_op | source)
XLA Modules:
  0.0 96.6 jit_solution(5173531013970896090)
XLA Ops:
  0.0 89.0 %update_parts.1 = (f32[512,512]{1,0:T(8,128)}, f32[1024,512]{1,0:T(8,128)}, f32[512,512]{1,0:T(8,128)}) custom-call(f32[1024,512]{1,0:T(8,128)} %prior_ref.1, s32[1,512]{1,0:T(1,128)} %bitcast.8, f32[1,512]{1,0:T(1,128)} %bitcast.9), custom_call_target="tpu_custom_call" | custom-call | tf_op jit(solution)/shard_map/update_parts/pallas_call | solution.py:285
  89.0 0.0 copy-start.1
  89.1 0.0 copy-start.2
  89.1 2.7 %fusion = f32[512,512]{1,0:T(8,128)S(1)} fusion(f32[512,512]{1,0:T(8,128)} %get-tuple-element.9, f32[512,512]{1,0:T(8,128)} %get-tuple-element.10), kind=kOutput, calls=%fused_computation.1 | convolution fusion | flops 805306368 | bytes 3145728 | tf_op jit(solution)/shard_map/dot_general | solution.py:312
  91.8 0.0 copy-done.1
  91.8 0.0 copy-start
  91.8 1.0 %fusion.1 = f32[512,512]{1,0:T(8,128)S(1)} fusion(f32[512,512]{1,0:T(8,128)S(1)} %copy-done.1, f32[512,512]{1,0:T(8,128)S(1)} %fusion), kind=kOutput, calls=%fused_computation.2 | convolution fusion | flops 805306368 | bytes 3145728 | tf_op jit(solution)/shard_map/dot_general | solution.py:313
  92.8 0.0 copy-done.2
  92.8 0.5 copy-done
  93.4 3.3 %convolution_subtract_fusion = f32[1024,512]{1,0:T(8,128)} fusion(f32[1024,512]{1,0:T(8,128)S(1)} %copy-done, f32[1024,512]{1,0:T(8,128)S(1)} %copy-done.2, f32[512,512]{1,0:T(8,128)S(1)} %fusion.1), kind=kOutput, calls=%fused_computation | convolution fusion | flops 1611137024 | bytes 7340032 | tf_op jit(solution)/shard_map/dot_general | solution.py:314
Async XLA Ops:
  89.0 2.7 %copy-start.1 = (f32[512,512]{1,0:T(8,128)S(1)}, f32[512,512]{1,0:T(8,128)}, u32[]{:S(2)}) copy-start(f32[512,512]{1,0:T(8,128)} %get-tuple-element.9) | copy-start | bytes 3145732
  89.1 3.8 %copy-start.2 = (f32[1024,512]{1,0:T(8,128)S(1)}, f32[1024,512]{1,0:T(8,128)}, u32[]{:S(2)}) copy-start(f32[1024,512]{1,0:T(8,128)} %get-tuple-element.8) | copy-start | bytes 6291460
  91.8 1.6 %copy-start = (f32[1024,512]{1,0:T(8,128)S(1)}, f32[1024,512]{1,0:T(8,128)}, u32[]{:S(2)}) copy-start(f32[1024,512]{1,0:T(8,128)} %prior_ref.1) | copy-start | bytes 6291460

commit v3 on v2

--- a/solution.py
+++ b/solution.py
@@ -225,27 +225,43 @@
     a_plans = [plan(a_part, a_ref, a_acc, (i * width, width), col_axes[i], []) for i in range(2)]
     b_plan = plan(b_part, b_ref, b_acc, (0, b_part.shape[1]), row_axes, [])
 
+    nc, nr = len(col_bits), len(row_bits)
+    early = min(2, nr)
     for step in range(len(s_plans[0])):
         for steps in s_plans:
             steps[step][0]()
-        if step == len(col_bits) + len(row_bits):
+        if step == 0:
             b_plan[0][0]()
         if step < 2:
             half = prior_ref.shape[0] // TILE // 2
             pick_columns(prior_ref, one_ref, a_part, step * half, (step + 1) * half)
+        if nc <= step < nc + early:
+            for steps in a_plans:
+                steps[step - nc][0]()
+        if step == nc + nr:
+            b_plan[1][0]()
         for steps in s_plans:
             steps[step][1]()
+        if step == nc - 1:
+            b_plan[0][1]()
+        if nc <= step < nc + early:
+            for steps in a_plans:
+                steps[step - nc][1]()
 
     total = TICKS * (obs // NB)
     actions = [[] for _ in range(total + 1)]
-    for steps, span, begun in [(a_plans[0], total, False), (a_plans[1], total, False), (b_plan, total - 1, True)]:
-        if not begun:
-            actions[0].append(steps[0][0])
-        for index in range(len(steps)):
-            slot = actions[round(span * (index + 1) / len(steps))]
-            slot.append(steps[index][1])
-            if index + 1 < len(steps):
-                slot.append(steps[index + 1][0])
+    for steps in a_plans:
+        left = steps[early:]
+        actions[0].append(left[0][0])
+        for index in range(len(left)):
+            slot = actions[round((total - 1) * (index + 1) / len(left))]
+            slot.append(left[index][1])
+            slot += [step[0] for step in left[index + 1:index + 2]]
+    left = b_plan[1:]
+    for index in range(len(left)):
+        slot = actions[1 + round((total - 1) * index / (len(left) - 1))]
+        slot.append(left[index][1])
+        slot += [step[0] for step in left[index + 1:index + 2]]
 
     i = lax.broadcasted_iota(jnp.int32, (obs, obs), 0)
     j = lax.broadcasted_iota(jnp.int32, (obs, obs), 1)

time: 96.8 us -> 85 us (0.88)
  Pallas kernels: 89 us -> 77.3 us
    pallas_call x1, Pallas kernels: 89 us -> 77.3 us  [update_parts(): pl.pallas_call(functools.partial(update_kernel, col_bits, row_bits), name...]
where the time goes in v3:
time: 85 us; the launch traced here: 84.9 us
  Pallas kernels  77.3 us (91%)
  matrix products  6.98 us (8%)
    pallas_call x1, Pallas kernels, update_parts(): pl.pallas_call(functools.partial(update_kernel, col_bits, row_bits), name...  77.3 us
    dot_general x1, matrix products, local(): return prior - jnp.dot(a, y, precision=MID, preferred_element_type=F32)  3.26 us
    dot_general x1, matrix products, local(): v = jnp.dot(linv, b, precision=MID, preferred_element_type=F32)  2.69 us

profile of v3, /device:TPU:0, one launch (start us, length us, event | category | flops | bytes accessed | tf_op | source)
XLA Modules:
  0.0 84.9 jit_solution(6023172330137959409)
XLA Ops:
  0.0 77.3 %update_parts.1 = (f32[512,512]{1,0:T(8,128)}, f32[1024,512]{1,0:T(8,128)}, f32[512,512]{1,0:T(8,128)}) custom-call(f32[1024,512]{1,0:T(8,128)} %prior_ref.1, s32[1,512]{1,0:T(1,128)} %bitcast.8, f32[1,512]{1,0:T(1,128)} %bitcast.9), custom_call_target="tpu_custom_call" | custom-call | tf_op jit(solution)/shard_map/update_parts/pallas_call | solution.py:301
  77.3 0.0 copy-start.1
  77.3 0.0 copy-start.2
  77.3 2.7 %fusion = f32[512,512]{1,0:T(8,128)S(1)} fusion(f32[512,512]{1,0:T(8,128)} %get-tuple-element.9, f32[512,512]{1,0:T(8,128)} %get-tuple-element.10), kind=kOutput, calls=%fused_computation.1 | convolution fusion | flops 805306368 | bytes 3145728 | tf_op jit(solution)/shard_map/dot_general | solution.py:328
  80.0 0.0 copy-done.1
  80.0 0.0 copy-start
  80.0 1.0 %fusion.1 = f32[512,512]{1,0:T(8,128)S(1)} fusion(f32[512,512]{1,0:T(8,128)S(1)} %copy-done.1, f32[512,512]{1,0:T(8,128)S(1)} %fusion), kind=kOutput, calls=%fused_computation.2 | convolution fusion | flops 805306368 | bytes 3145728 | tf_op jit(solution)/shard_map/dot_general | solution.py:329
  81.1 0.0 copy-done.2
  81.1 0.5 copy-done
  81.6 3.3 %convolution_subtract_fusion = f32[1024,512]{1,0:T(8,128)} fusion(f32[1024,512]{1,0:T(8,128)S(1)} %copy-done, f32[1024,512]{1,0:T(8,128)S(1)} %copy-done.2, f32[512,512]{1,0:T(8,128)S(1)} %fusion.1), kind=kOutput, calls=%fused_computation | convolution fusion | flops 1611137024 | bytes 7340032 | tf_op jit(solution)/shard_map/dot_general | solution.py:330
Async XLA Ops:
  77.3 2.7 %copy-start.1 = (f32[512,512]{1,0:T(8,128)S(1)}, f32[512,512]{1,0:T(8,128)}, u32[]{:S(2)}) copy-start(f32[512,512]{1,0:T(8,128)} %get-tuple-element.9) | copy-start | bytes 3145732
  77.3 3.8 %copy-start.2 = (f32[1024,512]{1,0:T(8,128)S(1)}, f32[1024,512]{1,0:T(8,128)}, u32[]{:S(2)}) copy-start(f32[1024,512]{1,0:T(8,128)} %get-tuple-element.8) | copy-start | bytes 6291460
  80.0 1.6 %copy-start = (f32[1024,512]{1,0:T(8,128)S(1)}, f32[1024,512]{1,0:T(8,128)}, u32[]{:S(2)}) copy-start(f32[1024,512]{1,0:T(8,128)} %prior_ref.1) | copy-start | bytes 6291460

commit v4 on v3

--- a/solution.py
+++ b/solution.py
@@ -61,7 +61,26 @@
         at = pl.ds(pl.multiple_of(t * TILE, TILE), TILE)
         g1, g2, g3 = parts3(b_ref[at, :])
         pick = one_ref[...]
-        s_ref[at, :] = dot(g1, pick) + dot(g2, pick) + dot(g3, pick)
+        s_ref[at, :obs] = dot(g1, pick) + dot(g2, pick) + dot(g3, pick)
+
+
+def packed_blocks(obs):
+    q = obs // 4
+    h = q // 2
+    return [
+        ((0, q, 0, obs), (0, 0)),
+        ((q, q, q, obs - q), (q, q)),
+        ((q, q, 0, q), (3 * q, 3 * q)),
+        ((2 * q, h, 0, 2 * q), (2 * q, 2 * q)),
+        ((2 * q, h, 2 * q, 2 * q), (2 * q + h, 2 * q)),
+    ]
+
+
+def halvings(rows, col_bits):
+    count = 0
+    while count < len(col_bits) and (rows >> (count + 1)) % 8 == 0:
+        count += 1
+    return count
 
 
 def pick_columns(prior_ref, one_ref, a_ref, first, last):
@@ -205,9 +224,11 @@
 def update_kernel(col_bits, row_bits, prior_ref, obs_ref, noise_ref, inv_ref, a_ref, b_ref, s_part, a_part, b_part, one_ref,
                   s_ref, sm, *rest):
     send_sem, recv_sem = rest[-2:]
-    pick_rows(prior_ref, obs_ref, one_ref, s_part, b_part)
+    obs = obs_ref.shape[1]
+    pick_rows(prior_ref, obs_ref, one_ref, sm, b_part)
+    for (r, n, c, w), (y, x) in packed_blocks(obs):
+        s_part[r:r + n, c:c + w] = sm[y:y + n, x:x + w]
     (s_acc, a_acc, b_acc), bufs = rest[:3], list(rest[3:-2])
-    obs = s_part.shape[0]
     col_axes = [[("col", b) for b in order] for order in orders(col_bits)]
     row_axes = [("row", b) for b in row_bits]
     greet(col_axes[0] + row_axes)
@@ -221,9 +242,13 @@
         return steps
 
     width = obs // 2
-    s_plans = [plan(s_part, s_ref, s_acc, (i * width, width), col_axes[i], row_axes) for i in range(2)]
+    cut = halvings(s_part.shape[0], col_bits)
+    s_plans = [
+        plan(s_part, s_ref, s_acc, (i * width, width), col_axes[i][:cut], col_axes[i][cut:] + row_axes) for i in range(2)
+    ]
     a_plans = [plan(a_part, a_ref, a_acc, (i * width, width), col_axes[i], []) for i in range(2)]
-    b_plan = plan(b_part, b_ref, b_acc, (0, b_part.shape[1]), row_axes, [])
+    wide = b_part.shape[1] // 2
+    b_plans = [plan(b_part, b_ref, b_acc, (i * wide, wide), row_axes, []) for i in range(2)]
 
     nc, nr = len(col_bits), len(row_bits)
     early = min(2, nr)
@@ -231,7 +256,8 @@
         for steps in s_plans:
             steps[step][0]()
         if step == 0:
-            b_plan[0][0]()
+            for steps in b_plans:
+                steps[0][0]()
         if step < 2:
             half = prior_ref.shape[0] // TILE // 2
             pick_columns(prior_ref, one_ref, a_part, step * half, (step + 1) * half)
@@ -239,11 +265,13 @@
             for steps in a_plans:
                 steps[step - nc][0]()
         if step == nc + nr:
-            b_plan[1][0]()
+            for steps in b_plans:
+                steps[1][0]()
         for steps in s_plans:
             steps[step][1]()
         if step == nc - 1:
-            b_plan[0][1]()
+            for steps in b_plans:
+                steps[0][1]()
         if nc <= step < nc + early:
             for steps in a_plans:
                 steps[step - nc][1]()
@@ -257,15 +285,19 @@
             slot = actions[round((total - 1) * (index + 1) / len(left))]
             slot.append(left[index][1])
             slot += [step[0] for step in left[index + 1:index + 2]]
-    left = b_plan[1:]
-    for index in range(len(left)):
-        slot = actions[1 + round((total - 1) * index / (len(left) - 1))]
-        slot.append(left[index][1])
-        slot += [step[0] for step in left[index + 1:index + 2]]
+    for stream, steps in enumerate(b_plans):
+        left = steps[1:]
+        for index in range(len(left)):
+            slot = actions[round(total * (2 * index + stream) / (2 * len(left) - 1))]
+            slot.append(left[index][1])
+            slot += [step[0] for step in left[index + 1:index + 2]]
 
     i = lax.broadcasted_iota(jnp.int32, (obs, obs), 0)
     j = lax.broadcasted_iota(jnp.int32, (obs, obs), 1)
-    sm[:, :obs] = s_ref[...] + jnp.where(i == j, noise_ref[...], 0.0)
+    sm[:, :obs] = jnp.zeros((obs, obs), F32)
+    for (r, n, c, w), (y, x) in packed_blocks(obs):
+        sm[y:y + n, x:x + w] = s_ref[r:r + n, c:c + w]
+    sm[:, :obs] += jnp.where(i == j, noise_ref[...], 0.0)
     sm[:, obs:] = jnp.where(i == j, 1.0, 0.0)
     eye = jnp.where(i[:NB, :NB] == j[:NB, :NB], 1.0, 0.0).astype(F32)
     wide = lax.broadcasted_iota(jnp.int32, (NB, obs), 1)
@@ -296,7 +328,9 @@
     (rows, cols), obs = prior.shape, observed.shape[0]
     col_bits, row_bits = bits(mesh.shape["col"]), bits(mesh.shape["row"])
     nc, nr = len(col_bits), len(row_bits)
-    copies = 2 * (2 * nc + nr) + 2 * 2 * nc + 2 * nr
+    packed = 5 * obs // 8
+    cut = halvings(packed, col_bits)
+    copies = 2 * (nc + cut + nr) + 2 * 2 * nc + 2 * 2 * nr
     like = jax.ShapeDtypeStruct
     return pl.pallas_call(
         functools.partial(update_kernel, col_bits, row_bits),
@@ -305,19 +339,19 @@
         in_specs=[VMEM] * 3,
         out_specs=(VMEM,) * 3,
         scratch_shapes=[
-            pltpu.VMEM((obs, obs), F32),
+            pltpu.VMEM((packed, obs), F32),
             pltpu.VMEM((rows, obs), F32),
             pltpu.VMEM((obs, cols), F32),
             pltpu.VMEM((cols, obs), BF16),
-            pltpu.VMEM((obs, obs), F32),
+            pltpu.VMEM((packed, obs), F32),
             pltpu.VMEM((obs, 2 * obs), F32),
-            pltpu.VMEM((obs, obs), F32),
+            pltpu.VMEM((packed, obs), F32),
             pltpu.VMEM((rows, obs), F32),
             pltpu.VMEM((obs, cols), F32),
         ]
-        + recv_shapes(obs, obs // 2, nc, nr) * 2
+        + recv_shapes(packed, obs // 2, cut, nc - cut + nr) * 2
         + recv_shapes(rows, obs // 2, nc, 0) * 2
-        + recv_shapes(obs, cols, nr, 0)
+        + recv_shapes(obs, cols // 2, nr, 0) * 2
         + [pltpu.SemaphoreType.DMA((copies,)), pltpu.SemaphoreType.DMA((copies,))],
         compiler_params=pltpu.CompilerParams(collective_id=0, has_side_effects=True, vmem_limit_bytes=LIMIT),
     )(prior, observed[None, :], noise[None, :])

time: 85 us -> 86.6 us (1.019)
  Pallas kernels: 77.3 us -> 78.8 us
    pallas_call x1, Pallas kernels: 77.3 us -> 78.8 us  [update_parts(): pl.pallas_call(functools.partial(update_kernel, col_bits, row_bits), name...]
where the time goes in v4:
time: 86.6 us; the launch traced here: 86.4 us
  Pallas kernels  78.8 us (91%)
  matrix products  6.97 us (8%)
    pallas_call x1, Pallas kernels, update_parts(): pl.pallas_call(functools.partial(update_kernel, col_bits, row_bits), name...  78.8 us
    dot_general x1, matrix products, local(): return prior - jnp.dot(a, y, precision=MID, preferred_element_type=F32)  3.26 us
    dot_general x1, matrix products, local(): v = jnp.dot(linv, b, precision=MID, preferred_element_type=F32)  2.69 us

profile of v4, /device:TPU:0, one launch (start us, length us, event | category | flops | bytes accessed | tf_op | source)
XLA Modules:
  0.0 86.4 jit_solution(9931150495353406508)
XLA Ops:
  0.0 78.8 %update_parts.1 = (f32[512,512]{1,0:T(8,128)}, f32[1024,512]{1,0:T(8,128)}, f32[512,512]{1,0:T(8,128)}) custom-call(f32[1024,512]{1,0:T(8,128)} %prior_ref.1, s32[1,512]{1,0:T(1,128)} %bitcast.8, f32[1,512]{1,0:T(1,128)} %bitcast.9), custom_call_target="tpu_custom_call" | custom-call | tf_op jit(solution)/shard_map/update_parts/pallas_call | solution.py:335
  78.8 0.0 copy-start.1
  78.8 0.0 copy-start.2
  78.8 2.7 %fusion = f32[512,512]{1,0:T(8,128)S(1)} fusion(f32[512,512]{1,0:T(8,128)} %get-tuple-element.9, f32[512,512]{1,0:T(8,128)} %get-tuple-element.10), kind=kOutput, calls=%fused_computation.1 | convolution fusion | flops 805306368 | bytes 3145728 | tf_op jit(solution)/shard_map/dot_general | solution.py:362
  81.5 0.0 copy-done.1
  81.5 0.0 copy-start
  81.6 1.0 %fusion.1 = f32[512,512]{1,0:T(8,128)S(1)} fusion(f32[512,512]{1,0:T(8,128)S(1)} %copy-done.1, f32[512,512]{1,0:T(8,128)S(1)} %fusion), kind=kOutput, calls=%fused_computation.2 | convolution fusion | flops 805306368 | bytes 3145728 | tf_op jit(solution)/shard_map/dot_general | solution.py:363
  82.6 0.0 copy-done.2
  82.6 0.5 copy-done
  83.1 3.3 %convolution_subtract_fusion = f32[1024,512]{1,0:T(8,128)} fusion(f32[1024,512]{1,0:T(8,128)S(1)} %copy-done, f32[1024,512]{1,0:T(8,128)S(1)} %copy-done.2, f32[512,512]{1,0:T(8,128)S(1)} %fusion.1), kind=kOutput, calls=%fused_computation | convolution fusion | flops 1611137024 | bytes 7340032 | tf_op jit(solution)/shard_map/dot_general | solution.py:364
Async XLA Ops:
  78.8 2.7 %copy-start.1 = (f32[512,512]{1,0:T(8,128)S(1)}, f32[512,512]{1,0:T(8,128)}, u32[]{:S(2)}) copy-start(f32[512,512]{1,0:T(8,128)} %get-tuple-element.9) | copy-start | bytes 3145732
  78.8 3.8 %copy-start.2 = (f32[1024,512]{1,0:T(8,128)S(1)}, f32[1024,512]{1,0:T(8,128)}, u32[]{:S(2)}) copy-start(f32[1024,512]{1,0:T(8,128)} %get-tuple-element.8) | copy-start | bytes 6291460
  81.5 1.6 %copy-start = (f32[1024,512]{1,0:T(8,128)S(1)}, f32[1024,512]{1,0:T(8,128)}, u32[]{:S(2)}) copy-start(f32[1024,512]{1,0:T(8,128)} %prior_ref.1) | copy-start | bytes 6291460

commit v5 on v4

--- a/solution.py
+++ b/solution.py
@@ -248,7 +248,8 @@
     ]
     a_plans = [plan(a_part, a_ref, a_acc, (i * width, width), col_axes[i], []) for i in range(2)]
     wide = b_part.shape[1] // 2
-    b_plans = [plan(b_part, b_ref, b_acc, (i * wide, wide), row_axes, []) for i in range(2)]
+    b_plans = [plan(b_part, b_ref, b_acc, (i * wide, wide), order, [])
+               for i, order in enumerate((row_axes, row_axes[::-1]))]
 
     nc, nr = len(col_bits), len(row_bits)
     early = min(2, nr)
@@ -285,10 +286,10 @@
             slot = actions[round((total - 1) * (index + 1) / len(left))]
             slot.append(left[index][1])
             slot += [step[0] for step in left[index + 1:index + 2]]
-    for stream, steps in enumerate(b_plans):
+    for steps in b_plans:
         left = steps[1:]
         for index in range(len(left)):
-            slot = actions[round(total * (2 * index + stream) / (2 * len(left) - 1))]
+            slot = actions[1 + round((total - 1) * (index / (len(left) - 1)) ** 1.5)]
             slot.append(left[index][1])
             slot += [step[0] for step in left[index + 1:index + 2]]
 

time: 86.6 us -> 84.7 us (0.978)
  Pallas kernels: 78.8 us -> 76.9 us
    pallas_call x1, Pallas kernels: 78.8 us -> 76.9 us  [update_parts(): pl.pallas_call(functools.partial(update_kernel, col_bits, row_bits), name...]
where the time goes in v5:
time: 84.7 us; the launch traced here: 84.5 us
  Pallas kernels  76.9 us (91%)
  matrix products  6.97 us (8%)
    pallas_call x1, Pallas kernels, update_parts(): pl.pallas_call(functools.partial(update_kernel, col_bits, row_bits), name...  76.9 us
    dot_general x1, matrix products, local(): return prior - jnp.dot(a, y, precision=MID, preferred_element_type=F32)  3.26 us
    dot_general x1, matrix products, local(): v = jnp.dot(linv, b, precision=MID, preferred_element_type=F32)  2.69 us

profile of v5, /device:TPU:0, one launch (start us, length us, event | category | flops | bytes accessed | tf_op | source)
XLA Modules:
  0.0 84.5 jit_solution(17147203588495514761)
XLA Ops:
  0.0 76.9 %update_parts.1 = (f32[512,512]{1,0:T(8,128)}, f32[1024,512]{1,0:T(8,128)}, f32[512,512]{1,0:T(8,128)}) custom-call(f32[1024,512]{1,0:T(8,128)} %prior_ref.1, s32[1,512]{1,0:T(1,128)} %bitcast.8, f32[1,512]{1,0:T(1,128)} %bitcast.9), custom_call_target="tpu_custom_call" | custom-call | tf_op jit(solution)/shard_map/update_parts/pallas_call | solution.py:336
  76.9 0.0 copy-start.1
  76.9 0.0 copy-start.2
  76.9 2.7 %fusion = f32[512,512]{1,0:T(8,128)S(1)} fusion(f32[512,512]{1,0:T(8,128)} %get-tuple-element.9, f32[512,512]{1,0:T(8,128)} %get-tuple-element.10), kind=kOutput, calls=%fused_computation.1 | convolution fusion | flops 805306368 | bytes 3145728 | tf_op jit(solution)/shard_map/dot_general | solution.py:363
  79.6 0.0 copy-done.1
  79.6 0.0 copy-start
  79.7 1.0 %fusion.1 = f32[512,512]{1,0:T(8,128)S(1)} fusion(f32[512,512]{1,0:T(8,128)S(1)} %copy-done.1, f32[512,512]{1,0:T(8,128)S(1)} %fusion), kind=kOutput, calls=%fused_computation.2 | convolution fusion | flops 805306368 | bytes 3145728 | tf_op jit(solution)/shard_map/dot_general | solution.py:364
  80.7 0.0 copy-done.2
  80.7 0.5 copy-done
  81.2 3.3 %convolution_subtract_fusion = f32[1024,512]{1,0:T(8,128)} fusion(f32[1024,512]{1,0:T(8,128)S(1)} %copy-done, f32[1024,512]{1,0:T(8,128)S(1)} %copy-done.2, f32[512,512]{1,0:T(8,128)S(1)} %fusion.1), kind=kOutput, calls=%fused_computation | convolution fusion | flops 1611137024 | bytes 7340032 | tf_op jit(solution)/shard_map/dot_general | solution.py:365
Async XLA Ops:
  76.9 2.7 %copy-start.1 = (f32[512,512]{1,0:T(8,128)S(1)}, f32[512,512]{1,0:T(8,128)}, u32[]{:S(2)}) copy-start(f32[512,512]{1,0:T(8,128)} %get-tuple-element.9) | copy-start | bytes 3145732
  76.9 3.8 %copy-start.2 = (f32[1024,512]{1,0:T(8,128)S(1)}, f32[1024,512]{1,0:T(8,128)}, u32[]{:S(2)}) copy-start(f32[1024,512]{1,0:T(8,128)} %get-tuple-element.8) | copy-start | bytes 6291460
  79.6 1.6 %copy-start = (f32[1024,512]{1,0:T(8,128)S(1)}, f32[1024,512]{1,0:T(8,128)}, u32[]{:S(2)}) copy-start(f32[1024,512]{1,0:T(8,128)} %prior_ref.1) | copy-start | bytes 6291460

commit v6 on v5

--- a/solution.py
+++ b/solution.py
@@ -270,10 +270,10 @@
                 steps[1][0]()
         for steps in s_plans:
             steps[step][1]()
-        if step == nc - 1:
+        if step == nc:
             for steps in b_plans:
                 steps[0][1]()
-        if nc <= step < nc + early:
+        if nc <= step < nc + early - 1:
             for steps in a_plans:
                 steps[step - nc][1]()
 
@@ -281,7 +281,7 @@
     actions = [[] for _ in range(total + 1)]
     for steps in a_plans:
         left = steps[early:]
-        actions[0].append(left[0][0])
+        actions[0] += [steps[early - 1][1], left[0][0]]
         for index in range(len(left)):
             slot = actions[round((total - 1) * (index + 1) / len(left))]
             slot.append(left[index][1])

time: 84.7 us -> 81.8 us (0.966)
  Pallas kernels: 76.9 us -> 74 us
    pallas_call x1, Pallas kernels: 76.9 us -> 74 us  [update_parts(): pl.pallas_call(functools.partial(update_kernel, col_bits, row_bits), name...]
where the time goes in v6:
time: 81.8 us; the launch traced here: 81.6 us
  Pallas kernels  74 us (90%)
  matrix products  6.97 us (9%)
    pallas_call x1, Pallas kernels, update_parts(): pl.pallas_call(functools.partial(update_kernel, col_bits, row_bits), name...  74 us
    dot_general x1, matrix products, local(): return prior - jnp.dot(a, y, precision=MID, preferred_element_type=F32)  3.26 us
    dot_general x1, matrix products, local(): v = jnp.dot(linv, b, precision=MID, preferred_element_type=F32)  2.69 us

profile of v6, /device:TPU:0, one launch (start us, length us, event | category | flops | bytes accessed | tf_op | source)
XLA Modules:
  0.0 81.6 jit_solution(15308736451297350716)
XLA Ops:
  0.0 74.0 %update_parts.1 = (f32[512,512]{1,0:T(8,128)}, f32[1024,512]{1,0:T(8,128)}, f32[512,512]{1,0:T(8,128)}) custom-call(f32[1024,512]{1,0:T(8,128)} %prior_ref.1, s32[1,512]{1,0:T(1,128)} %bitcast.8, f32[1,512]{1,0:T(1,128)} %bitcast.9), custom_call_target="tpu_custom_call" | custom-call | tf_op jit(solution)/shard_map/update_parts/pallas_call | solution.py:336
  74.0 0.0 copy-start.1
  74.0 0.0 copy-start.2
  74.1 2.7 %fusion = f32[512,512]{1,0:T(8,128)S(1)} fusion(f32[512,512]{1,0:T(8,128)} %get-tuple-element.9, f32[512,512]{1,0:T(8,128)} %get-tuple-element.10), kind=kOutput, calls=%fused_computation.1 | convolution fusion | flops 805306368 | bytes 3145728 | tf_op jit(solution)/shard_map/dot_general | solution.py:363
  76.8 0.0 copy-done.1
  76.8 0.0 copy-start
  76.8 1.0 %fusion.1 = f32[512,512]{1,0:T(8,128)S(1)} fusion(f32[512,512]{1,0:T(8,128)S(1)} %copy-done.1, f32[512,512]{1,0:T(8,128)S(1)} %fusion), kind=kOutput, calls=%fused_computation.2 | convolution fusion | flops 805306368 | bytes 3145728 | tf_op jit(solution)/shard_map/dot_general | solution.py:364
  77.8 0.0 copy-done.2
  77.8 0.5 copy-done
  78.4 3.3 %convolution_subtract_fusion = f32[1024,512]{1,0:T(8,128)} fusion(f32[1024,512]{1,0:T(8,128)S(1)} %copy-done, f32[1024,512]{1,0:T(8,128)S(1)} %copy-done.2, f32[512,512]{1,0:T(8,128)S(1)} %fusion.1), kind=kOutput, calls=%fused_computation | convolution fusion | flops 1611137024 | bytes 7340032 | tf_op jit(solution)/shard_map/dot_general | solution.py:365
Async XLA Ops:
  74.0 2.7 %copy-start.1 = (f32[512,512]{1,0:T(8,128)S(1)}, f32[512,512]{1,0:T(8,128)}, u32[]{:S(2)}) copy-start(f32[512,512]{1,0:T(8,128)} %get-tuple-element.9) | copy-start | bytes 3145732
  74.0 3.8 %copy-start.2 = (f32[1024,512]{1,0:T(8,128)S(1)}, f32[1024,512]{1,0:T(8,128)}, u32[]{:S(2)}) copy-start(f32[1024,512]{1,0:T(8,128)} %get-tuple-element.8) | copy-start | bytes 6291460
  76.8 1.6 %copy-start = (f32[1024,512]{1,0:T(8,128)S(1)}, f32[1024,512]{1,0:T(8,128)}, u32[]{:S(2)}) copy-start(f32[1024,512]{1,0:T(8,128)} %prior_ref.1) | copy-start | bytes 6291460
